TPU v7x, 256 devices: a whole 4x4x8 slice. The times are simulated.
256 devices in a mesh: dp: 128 (over y, z, x), tensor: 2 (over core).
Axes of the slice: x: 4, y: 4, z: 8, core: 2. Of those that a mesh axis runs over, the one named last changes fastest.
Arguments:
- queries: bfloat16 [16384, 4096], P('dp', 'tensor'), may hold values from -4 to 4
- cached_key_rows: bfloat16 [256, 1024, 1024], P('dp', None, 'tensor'), may hold values from -1 to 1
- cached_value_rows: bfloat16 [256, 1024, 1024], P('dp', None, 'tensor'), may hold values from -6 to 6
- parent_ids: int32 [16384], P('dp'), may hold values from 0 to 255, as said below
- lengths: int32 [256], P('dp'), may hold values from 128 to 1024
- residual: bfloat16 [16384, 2048], P('dp', 'tensor'), may hold values from -4 to 4
- out_weight: bfloat16 [4096, 2048], P('tensor'), may hold values from -0.09375 to 0.09375
Outputs:
- mixed_out: bfloat16 [16384, 2048], P('dp', 'tensor')
Inputs may be any that keep to these rules, and one draw needn't show every extreme that they name: `parent_ids`: among the 128 children of one index of dp (aligned blocks), at most 2 have parents of one owner; in every draw one owner has exactly 2 children from every block.
All inputs are finite; a program needn't handle non-finite values.
Results may differ from a plain program's by a relative error of at most 0.0044.
Values may be sent and summed in bfloat16 or wider, within the bound.
No kernel may reach another device: no remote copies, remote signals or barrier semaphores. Data moves between devices by JAX's collectives and lax.ppermute only.
A program may use at most 64 MiB of HBM per device.

v0:
```python
import math

import jax
import jax.numpy as jnp
from jax import lax
from jax.sharding import PartitionSpec as P

HEAD_WIDTH = 128


def cut_along(value, dim, devices):
    dims = value.shape
    pieces = value.reshape(*dims[:dim], devices, dims[dim] // devices, *dims[dim + 1 :])
    return jnp.moveaxis(pieces, dim, 0)


def sent_and_summed(value, axis, dim):
    devices = lax.axis_size(axis)
    pieces = lax.all_to_all(cut_along(value, dim, devices), axis, 0, 0, tiled=True)
    return jnp.sum(pieces.astype(jnp.float32), axis=0)


def attend(rows, key_block, value_block, prefix_length, kv_heads):
    slot_total, columns = rows.shape
    group_width = columns // (kv_heads * HEAD_WIDTH)
    prefix_span = key_block.shape[0]
    query_head_count = rows.reshape(slot_total, kv_heads, group_width, HEAD_WIDTH)
    key_heads = key_block.reshape(prefix_span, kv_heads, HEAD_WIDTH)
    value_heads = value_block.reshape(prefix_span, kv_heads, HEAD_WIDTH)
    scores = jnp.einsum(
        "sjgd,ljd->jsgl", query_head_count, key_heads, preferred_element_type=jnp.float32
    )
    scores = scores * (1.0 / math.sqrt(HEAD_WIDTH))
    live_mask = jnp.arange(prefix_span, dtype=jnp.int32) < prefix_length
    raised = jnp.where(live_mask, jnp.exp(scores), jnp.zeros((), jnp.float32))
    totals = jnp.sum(raised, axis=-1)
    summed = jnp.einsum(
        "jsgl,ljd->sjgd",
        raised.astype(jnp.bfloat16),
        value_heads,
        preferred_element_type=jnp.float32,
    )
    scaled = summed / jnp.transpose(totals, (1, 0, 2))[..., None]
    return scaled.reshape(slot_total, columns).astype(jnp.bfloat16)


def local(queries, cached_key_rows, cached_value_rows, parent_ids, lengths, residual, out_weight):
    dp_count = lax.axis_size("dp")
    children = queries.shape[0]
    columns = queries.shape[1]
    kv_heads = cached_key_rows.shape[2] // HEAD_WIDTH
    parents_here = lengths.shape[0]
    capacity = max(2, 2 * children // dp_count)
    owner_of = parent_ids // parents_here
    sub_index = parent_ids % parents_here
    slot_count = dp_count * capacity
    order_rows = jnp.arange(children, dtype=jnp.int32)
    earlier = (owner_of[:, None] == owner_of[None, :]) & (order_rows[:, None] > order_rows[None, :])
    slot_rank = jnp.sum(earlier.astype(jnp.int32), axis=1)
    slot_of = owner_of * capacity + slot_rank
    placing = jnp.arange(slot_count, dtype=jnp.int32)[:, None] == slot_of[None, :]
    placing_rows = placing.astype(jnp.bfloat16)
    outgoing = jnp.dot(placing_rows, queries, preferred_element_type=jnp.float32).astype(
        jnp.bfloat16
    )
    slot_parent = jnp.sum(jnp.where(placing, sub_index[None, :] + 1, 0), axis=1) - 1
    arrived, arrived_parent = (
        lax.all_to_all(outgoing, "dp", split_axis=0, concat_axis=0, tiled=True),
        lax.all_to_all(slot_parent, "dp", split_axis=0, concat_axis=0, tiled=True),
    )
    answered = jnp.zeros((slot_count, columns), jnp.bfloat16)
    for parent in range(parents_here):
        answer = attend(
            arrived, cached_key_rows[parent], cached_value_rows[parent], lengths[parent], kv_heads
        )
        answered = jnp.where((arrived_parent == parent)[:, None], answer, answered)
    returned = lax.all_to_all(answered, "dp", split_axis=0, concat_axis=0, tiled=True)
    attended = lax.dot_general(
        placing_rows, returned, (((0,), (0,)), ((), ())), preferred_element_type=jnp.float32
    ).astype(jnp.bfloat16)
    partial_value = jnp.dot(attended, out_weight, preferred_element_type=jnp.float32)
    summed = sent_and_summed(partial_value.astype(jnp.bfloat16), "tensor", 1)
    return (residual.astype(jnp.float32) + summed).astype(jnp.bfloat16)


def solution(mesh):
    placed = (
        P("dp", "tensor"),
        P("dp", None, "tensor"),
        P("dp", None, "tensor"),
        P("dp"),
        P("dp"),
        P("dp", "tensor"),
        P("tensor", None),
    )
    return jax.shard_map(
        local, mesh=mesh, in_specs=placed, out_specs=P("dp", "tensor"), check_vma=False
    )
```

profile of v0, /device:TPU:1, one launch (start us, length us, event | category | flops | bytes accessed | tf_op | source)
XLA Modules:
  0.0 136.7 jit_solution(2214048519723608543)
XLA Ops:
  1.0 0.8 sub.13
  1.8 16.3 %all-to-all-start = ((s32[128,2,1]{1,2,0:T(1,128)}), s32[128,2,1]{1,2,0:T(1,128)S(1)}, u32[]{:S(2)}, u32[]{:S(2)}) async-start(s32[128,2,1]{1,2,0:T(1,128)} %bitcast), calls=%async_computation | async-start | bytes 131072 | tf_op jit(solution)/shard_map/all_to_all | solution.py:69
  18.6 1.5 %all_to_all.20 = bf16[128,2,2048]{2,1,0:T(2,128)(2,1)} reshape(bf16[256,2048]{1,0:T(8,128)(2,1)S(1)} %convolution_convert_fusion) | data formatting | bytes 2097152 | tf_op jit(solution)/shard_map/all_to_all | solution.py:68
  20.1 8.6 %all-to-all-done = s32[128,2,1]{1,2,0:T(1,128)S(1)} async-done(((s32[128,2,1]{1,2,0:T(1,128)}), s32[128,2,1]{1,2,0:T(1,128)S(1)}, u32[]{:S(2)}, u32[]{:S(2)}) %all-to-all-start) | async-done | bytes 1056 | tf_op jit(solution)/shard_map/all_to_all | solution.py:69
  28.7 6.4 %all-to-all-start.1 = ((bf16[128,2,2048]{2,1,0:T(2,128)(2,1)}), bf16[128,2,2048]{2,1,0:T(2,128)(2,1)S(1)}, u32[]{:S(2)}, u32[]{:S(2)}) async-start(bf16[128,2,2048]{2,1,0:T(2,128)(2,1)} %all_to_all.20), calls=%async_computation.1 | async-start | bytes 2097152 | tf_op jit(solution)/shard_map/all_to_all | solution.py:68
  35.1 2.7 %fusion.33 = (bf16[1,1024,512]{2,1,0:T(8,128)(2,1)}, bf16[1,1024,512]{2,1,0:T(8,128)(2,1)S(1)}) fusion(bf16[2,1024,512]{2,1,0:T(8,128)(2,1)} %param.8), kind=kLoop, calls=%fused_computation.53 | loop fusion | bytes 4194304 | tf_op jit(solution)/shard_map/slice | solution.py:74
  37.7 2.3 %copy.92 = bf16[1,1024,512]{1,2,0:T(8,128)(2,1)} copy(bf16[1,1024,512]{2,1,0:T(8,128)(2,1)} %get-tuple-element.5) | data formatting | bytes 2097152
  40.0 3.0 %fusion.34 = (bf16[1,1024,512]{2,1,0:T(8,128)(2,1)}, bf16[1,1024,512]{2,1,0:T(8,128)(2,1)}) fusion(bf16[2,1024,512]{2,1,0:T(8,128)(2,1)} %param.9), kind=kLoop, calls=%fused_computation.54 | loop fusion | bytes 4194304 | tf_op jit(solution)/shard_map/slice | solution.py:74
  43.0 2.3 %copy.93 = bf16[1,1024,512]{1,2,0:T(8,128)(2,1)} copy(bf16[1,1024,512]{2,1,0:T(8,128)(2,1)} %get-tuple-element.7) | data formatting | bytes 2097152
  45.3 1.3 copy.90
  46.6 2.4 %copy.91 = bf16[1,1024,512]{1,2,0:T(8,128)(2,1)} copy(bf16[1,1024,512]{2,1,0:T(8,128)(2,1)} %get-tuple-element.8) | data formatting | bytes 2097152
  51.4 9.9 %all-to-all-done.1 = bf16[128,2,2048]{2,1,0:T(2,128)(2,1)S(1)} async-done(((bf16[128,2,2048]{2,1,0:T(2,128)(2,1)}), bf16[128,2,2048]{2,1,0:T(2,128)(2,1)S(1)}, u32[]{:S(2)}, u32[]{:S(2)}) %all-to-all-start.1) | async-done | bytes 1048608 | tf_op jit(solution)/shard_map/all_to_all | solution.py:68
  61.2 1.5 %reshape.63 = bf16[256,4,4,128]{3,2,1,0:T(4,128)(2,1)} reshape(bf16[128,2,2048]{2,1,0:T(2,128)(2,1)S(1)} %all-to-all-done.1) | data formatting | bytes 2097152 | tf_op jit(solution)/shard_map/reshape | solution.py:27
  62.7 5.5 %fusion.2 = (f32[4,256,4]{1,2,0:T(4,128)S(1)}, f32[4,256,4,1024]{3,1,2,0:T(8,128)S(1)}) fusion(pred[1024]{0:T(1024)(128)(4,1)S(1)} %iota_compare_fusion.5, bf16[1024,4,128,1]{0,2,3,1:T(8,128)(2,1)} %bitcast.55, bf16[256,4,4,128]{3,2,1,0:T(4,128)(2,1)} %reshape.63), kind=kOutput, calls=%fused_computation.4 | convolution fusion | flops 1086320640 | bytes 18891776 | tf_op jit(solution)/shard_map/sjgd,ljd->jsgl/dot_general | solution.py:30
  68.2 3.2 %fusion.14 = bf16[256,4,4,128]{3,0,2,1:T(8,128)(2,1)S(1)} fusion(bf16[1024,4,128,1]{0,2,3,1:T(8,128)(2,1)S(1)} %bitcast.56, f32[4,256,4,1024]{3,1,2,0:T(8,128)S(1)} %get-tuple-element.18, pred[1024]{0:T(1024)(128)(4,1)S(1)} %iota_compare_fusion.5, f32[256,4,4]{0,2,1:T(4,128)S(1)} %bitcast.58), kind=kOutput, calls=%fused_computation.18 | convolution fusion | flops 1087373312 | bytes 18891776 | tf_op jit(solution)/shard_map/jsgl,ljd->sjgd/dot_general | solution.py:37
  71.4 0.8 copy.76
  72.5 5.5 %fusion = (f32[4,256,4]{1,2,0:T(4,128)S(1)}, f32[4,256,4,1024]{3,1,2,0:T(8,128)S(1)}) fusion(pred[1024]{0:T(1024)(128)(4,1)S(1)} %iota_compare_fusion.6, bf16[1024,4,128,1]{0,2,3,1:T(8,128)(2,1)} %bitcast.54, bf16[256,4,4,128]{3,2,1,0:T(4,128)(2,1)} %reshape.63), kind=kOutput, calls=%fused_computation.2 | convolution fusion | flops 1086320640 | bytes 18891776 | tf_op jit(solution)/shard_map/sjgd,ljd->jsgl/dot_general | solution.py:30
  78.0 4.0 %fusion.15 = bf16[256,4,4,128]{3,0,2,1:T(8,128)(2,1)S(1)} fusion(bf16[1024,4,128,1]{0,2,3,1:T(8,128)(2,1)} %bitcast.53, f32[4,256,4,1024]{3,1,2,0:T(8,128)S(1)} %get-tuple-element.16, pred[1024]{0:T(1024)(128)(4,1)S(1)} %iota_compare_fusion.6, f32[256,4,4]{0,2,1:T(4,128)S(1)} %bitcast.57), kind=kOutput, calls=%fused_computation.20 | convolution fusion | flops 1087373312 | bytes 18891776 | tf_op jit(solution)/shard_map/jsgl,ljd->sjgd/dot_general | solution.py:37
  82.1 1.8 %copy.68 = bf16[256,4,4,128]{3,2,1,0:T(4,128)(2,1)} copy(bf16[256,4,4,128]{3,0,2,1:T(8,128)(2,1)S(1)} %fusion.15) | data formatting | bytes 2097152 | tf_op jit(solution)/shard_map/convert_element_type | solution.py:44
  83.9 1.3 convert_element_type.47
  85.2 1.8 %broadcast_select_fusion.1 = bf16[128,2,2048]{2,1,0:T(2,128)(2,1)S(1)} fusion(bf16[128,2,2048]{2,1,0:T(2,128)(2,1)S(1)} %convert_element_type.47, pred[128,2]{1,0:T(8,128)(4,1)S(1)} %copy.62, bf16[128,2,2048]{2,1,0:T(2,128)(2,1)S(1)} %convert_element_type.50, pred[128,2]{1,0:T(8,128)(4,1)S(1)} %copy.70), kind=kLoop, calls=%fused_computation.22 | loop fusion | flops 1048576 | bytes 3146240 | tf_op jit(solution)/shard_map/jit(_where)/select_n | solution.py:76
  87.0 34.3 %all_to_all.29 = bf16[128,2,2048]{2,1,0:T(2,128)(2,1)S(1)} all-to-all(bf16[128,2,2048]{2,1,0:T(2,128)(2,1)S(1)} %broadcast_select_fusion.1), channel_id=1, replica_groups=mesh['dp'=128,'tensor'=2] {'dp'}, dimensions={0} | all-to-all | bytes 2097152 | tf_op jit(solution)/shard_map/all_to_all | solution.py:77
  121.8 4.8 %convolution_convert_fusion.1 = bf16[128,2048]{1,0:T(8,128)(2,1)S(1)} fusion(bf16[2048,2048]{1,0:T(8,128)(2,1)} %param.13, bf16[256,2048]{1,0:T(8,128)(2,1)S(1)} %all_to_all.23, s32[128]{0:T(128)S(1)} %multiply_add_fusion), kind=kOutput, calls=%fused_computation.15 | convolution fusion | flops 1208516608 | bytes 9961984 | tf_op jit(solution)/shard_map/dot_general | solution.py:81
  126.7 9.2 %all_to_all.30 = bf16[2,128,1024]{2,1,0:T(8,128)(2,1)S(1)} all-to-all(bf16[2,128,1024]{2,1,0:T(8,128)(2,1)S(1)} %bitcast.52), channel_id=1, replica_groups=mesh['dp'=128,'tensor'=2] {'tensor'}, dimensions={0} | all-to-all | bytes 1048576 | tf_op jit(solution)/shard_map/all_to_all | solution.py:19
  (28 shorter events, 5.4 us)
Async XLA Ops:
  0.0 18.2 %copy-start = (bf16[128,2048]{1,0:T(8,128)(2,1)S(1)}, bf16[128,2048]{1,0:T(8,128)(2,1)}, u32[]{:S(2)}) copy-start(bf16[128,2048]{1,0:T(8,128)(2,1)} %param.7) | copy-start | bytes 1572868
  0.0 49.0 %copy-start.4 = (s32[2]{0:T(128)S(1)}, s32[2]{0:T(128)}, u32[]{:S(2)}) copy-start(s32[2]{0:T(128)} %param.11) | copy-start | bytes 28
  1.8 26.9 %all-to-all-start = ((s32[128,2,1]{1,2,0:T(1,128)}), s32[128,2,1]{1,2,0:T(1,128)S(1)}, u32[]{:S(2)}, u32[]{:S(2)}) async-start(s32[128,2,1]{1,2,0:T(1,128)} %bitcast), calls=%async_computation | async-start | bytes 131072 | tf_op jit(solution)/shard_map/all_to_all | solution.py:69
  28.7 32.5 %all-to-all-start.1 = ((bf16[128,2,2048]{2,1,0:T(2,128)(2,1)}), bf16[128,2,2048]{2,1,0:T(2,128)(2,1)S(1)}, u32[]{:S(2)}, u32[]{:S(2)}) async-start(bf16[128,2,2048]{2,1,0:T(2,128)(2,1)} %all_to_all.20), calls=%async_computation.1 | async-start | bytes 2097152 | tf_op jit(solution)/shard_map/all_to_all | solution.py:68
  46.6 21.6 %copy-start.2 = (bf16[1,1024,512]{1,2,0:T(8,128)(2,1)S(1)}, bf16[1,1024,512]{1,2,0:T(8,128)(2,1)}, u32[]{:S(2)}) copy-start(bf16[1,1024,512]{1,2,0:T(8,128)(2,1)} %copy.93) | copy-start | bytes 3145732
  78.0 58.7 %copy-start.1 = (bf16[128,2048]{1,0:T(8,128)(2,1)S(1)}, bf16[128,2048]{1,0:T(8,128)(2,1)}, u32[]{:S(2)}) copy-start(bf16[128,2048]{1,0:T(8,128)(2,1)} %param.7) | copy-start | bytes 1572868
  82.1 53.9 %copy-start.3 = (bf16[128,1024]{1,0:T(8,128)(2,1)S(1)}, bf16[128,1024]{1,0:T(8,128)(2,1)}, u32[]{:S(2)}) copy-start(bf16[128,1024]{1,0:T(8,128)(2,1)} %param.12) | copy-start | bytes 786436
where the time goes:
time: 137 us
  blocking collectives  43.5 us (32%)
  local copies, waits for them, and re-layouts  23.4 us (17%)
  matrix products  23.4 us (17%)
  starting transfers between devices  22.7 us (17%)
  waiting for transfers between devices  18.4 us (13%)
  other arithmetic  5.04 us (4%)
    all_to_all x1, blocking collectives, local(): lax.all_to_all(answered, 'dp', split_axis=0, concat_axis=0, tiled=True)  34.3 us
    all_to_all x1, starting transfers between devices, local(): lax.all_to_all(slot_parent, 'dp', split_axis=0, concat_axis=0, tiled=True)  16.3 us
    dot_general x2, matrix products, attend(): jnp.einsum('sjgd,ljd->jsgl', query_head_count, key_heads, preferred_eleme...  11 us
    all_to_all x1, waiting for transfers between devices, local(): lax.all_to_all(outgoing, 'dp', split_axis=0, concat_axis=0, tiled=True)  9.86 us
    all_to_all x1, blocking collectives, sent_and_summed(): lax.all_to_all(cut_along(value, dim, devices), axis, 0, 0, tiled=True)  9.15 us
    all_to_all x1, waiting for transfers between devices, local(): lax.all_to_all(slot_parent, 'dp', split_axis=0, concat_axis=0, tiled=True)  8.59 us
    unnamed x14, local copies, waits for them, and re-layouts  8.25 us
    dot_general x2, matrix products, attend(): jnp.einsum('jsgl,ljd->sjgd', raised.astype(jnp.bfloat16), value_heads, pr...  7.19 us
  transfers between devices with their start and end apart: 2, of which 2 were waited for; matrix products, arithmetic and copies ran while one was open for 12% of the time, Pallas kernels for 0%

commit v1 on v0

v1 whole, which is shorter than its diff:
```python
import math

import jax
import jax.numpy as jnp
from jax import lax
from jax.experimental import pallas as pl
from jax.experimental.pallas import tpu as pltpu
from jax.sharding import PartitionSpec as P

HEAD_WIDTH = 128
LANES = 128
CHUNK = 64

F32 = jnp.float32
BF16 = jnp.bfloat16
VMEM = pl.BlockSpec(memory_space=pltpu.VMEM)
SMEM = pl.BlockSpec(memory_space=pltpu.SMEM)
ANY = pl.BlockSpec(memory_space=pl.ANY)
PARAMS = pltpu.CompilerParams(vmem_limit_bytes=56 * 1024 * 1024)


def iota(shape, dim):
    return lax.broadcasted_iota(jnp.int32, shape, dim)


def one_hot(flags):
    return jnp.where(flags, 1.0, 0.0).astype(BF16)


def product(left, right):
    return jnp.dot(left, right, preferred_element_type=F32)


def as_column(row):
    n = row.shape[1]
    eye = iota((n, n), 0) == iota((n, n), 1)
    return jnp.sum(jnp.where(eye, row, 0.0), axis=1, keepdims=True)


def as_row(column):
    n = column.shape[0]
    eye = iota((n, n), 0) == iota((n, n), 1)
    return jnp.sum(jnp.where(eye, column, 0.0), axis=0, keepdims=True)


def owners(ids, parents_here):
    shift = parents_here.bit_length() - 1
    owner = lax.shift_right_logical(ids, shift)
    return owner.astype(F32), (ids - lax.shift_left(owner, shift)).astype(F32)


def send_kernel(capacity, kv_heads, parents_here, ids_ref, queries_ref, out_ref):
    children = queries_ref.shape[0]
    width = queries_ref.shape[1] // kv_heads
    rows = out_ref.shape[0]
    owner, sub = owners(ids_ref[...], parents_here)
    owner_column = as_column(owner)
    square = (children, children)
    earlier = (owner_column == owner) & (iota(square, 0) < iota(square, 1))
    rank = jnp.sum(jnp.where(earlier, 1.0, 0.0), axis=0, keepdims=True)
    slot = (owner * capacity + rank).astype(jnp.int32)
    row = iota((rows, children), 0)
    shift = kv_heads.bit_length() - 1
    here = lax.shift_right_logical(row, shift) == slot
    head = row & (kv_heads - 1)
    placing = jnp.concatenate([one_hot(here & (head == j)) for j in range(kv_heads)], axis=1)
    stacked = jnp.concatenate(
        [queries_ref[:, j * width : (j + 1) * width] for j in range(kv_heads)], axis=0
    )
    out_ref[:, :width] = product(placing, stacked).astype(BF16)
    mark = jnp.broadcast_to(as_column(sub) + 1.0, (children, LANES)).astype(BF16)
    out_ref[:, width:] = product(one_hot(here), mark).astype(BF16)


def attend_kernel(
    capacity, kv_heads, lengths_ref, arrived_ref, keys_hbm, values_hbm, weight_hbm,
    attended_ref, partial_ref, keys, values, weight, natural, ordered, answered, sems,
):
    parents_here, prefix, _ = keys.shape
    sources = arrived_ref.shape[0] // (capacity * kv_heads)
    slots = sources * capacity
    width = arrived_ref.shape[1] - LANES
    group = width // HEAD_WIDTH
    half = weight.shape[1]
    other = pl.multiple_of((1 - lax.axis_index("tensor")) * half, half)
    copies = (
        pltpu.make_async_copy(keys_hbm, keys, sems.at[0]),
        pltpu.make_async_copy(values_hbm, values, sems.at[1]),
        pltpu.make_async_copy(weight_hbm.at[:, pl.ds(other, half)], weight, sems.at[2]),
    )
    for copy in copies:
        copy.start()
    rows = arrived_ref.shape[0]
    for j in range(kv_heads):
        place = iota((slots, rows), 0)
        source = place & (sources - 1)
        rank = lax.shift_right_logical(place, sources.bit_length() - 1)
        picked = one_hot(
            iota((slots, rows), 1) == source * (capacity * kv_heads) + rank * kv_heads + j
        )
        if j == 0:
            found = product(picked, arrived_ref[...])
            natural[:, :width] = found[:, :width].astype(BF16)
            marks = found[:, width:]
        else:
            natural[:, j * width : (j + 1) * width] = product(
                picked, arrived_ref[:, :width]
            ).astype(BF16)
    before = one_hot(iota((slots, slots), 0) > iota((slots, slots), 1))
    position = jnp.full((slots, LANES), -1.0, F32)
    start = jnp.int32(0)
    ends = []
    for parent in range(parents_here):
        mine = marks == parent + 1.0
        ahead = product(before, one_hot(mine))
        position = jnp.where(mine, ahead + start.astype(F32), position)
        count = (jnp.sum(jnp.where(mine, 1.0, 0.0)) * (1.0 / LANES)).astype(jnp.int32)
        start = start + lax.shift_left(
            lax.shift_right_logical(count + (CHUNK - 1), CHUNK.bit_length() - 1),
            CHUNK.bit_length() - 1,
        )
        ends.append(start)
    position_row = jnp.concatenate(
        [as_row(position[k * sources : (k + 1) * sources]) for k in range(capacity)], axis=1
    ).astype(jnp.int32)
    places = ordered.shape[0]
    ordering = one_hot(iota((places, slots), 0) == position_row)
    ordered[...] = product(ordering, natural[...]).astype(BF16)
    answered[...] = jnp.zeros_like(answered)
    copies[0].wait()
    copies[1].wait()
    factor = (1.0 / math.sqrt(HEAD_WIDTH)) * math.log2(math.e)

    def chunk_step(index, carry):
        base = pl.multiple_of(index * CHUNK, CHUNK)
        parent = jnp.int32(0)
        for end in ends[:-1]:
            parent = parent + (base >= end).astype(jnp.int32)
        live = iota((CHUNK * group, prefix), 1) < lengths_ref[parent]
        for j in range(kv_heads):
            block = ordered[pl.ds(base, CHUNK), j * width : (j + 1) * width]
            heads = jnp.concatenate(
                [block[:, g * HEAD_WIDTH : (g + 1) * HEAD_WIDTH] for g in range(group)], axis=0
            )
            columns = slice(j * HEAD_WIDTH, (j + 1) * HEAD_WIDTH)
            scores = lax.dot_general(
                heads, keys[parent, :, columns], (((1,), (1,)), ((), ())),
                preferred_element_type=F32,
            )
            raised = jnp.where(live, jnp.exp2(scores * factor), 0.0)
            totals = jnp.sum(raised, axis=1, keepdims=True)
            summed = product(raised.astype(BF16), values[parent, :, columns])
            scaled = (summed / totals).astype(BF16)
            for g in range(group):
                answered[
                    pl.ds(base, CHUNK),
                    j * width + g * HEAD_WIDTH : j * width + (g + 1) * HEAD_WIDTH,
                ] = scaled[g * CHUNK : (g + 1) * CHUNK]
        return carry

    lax.fori_loop(0, lax.shift_right_logical(start, CHUNK.bit_length() - 1), chunk_step, 0)
    lane = iota((slots, places), 1).astype(F32)
    back = one_hot(lane == position[:, :1])
    attended_ref[...] = product(back, answered[...]).astype(BF16)
    copies[2].wait()
    partial_ref[...] = product(attended_ref[...], weight[...]).astype(BF16)


def project_kernel(attended_ref, weight_hbm, out_ref, weight, sems):
    half = weight.shape[1]
    mine = pl.multiple_of(lax.axis_index("tensor") * half, half)
    parts = sems.shape[0]
    depth = weight.shape[0] // parts
    copies = [
        pltpu.make_async_copy(
            weight_hbm.at[pl.ds(i * depth, depth), pl.ds(mine, half)],
            weight.at[pl.ds(i * depth, depth)],
            sems.at[i],
        )
        for i in range(parts)
    ]
    for copy in copies:
        copy.start()
    for i, copy in enumerate(copies):
        copy.wait()
        rows = slice(i * depth, (i + 1) * depth)
        term = product(attended_ref[:, rows], weight[rows])
        out_ref[...] = term if i == 0 else out_ref[...] + term


def answer_kernel(capacity, parts, mine_ref, other_ref, out_ref):
    slots, columns = mine_ref.shape
    sources = slots // capacity
    width = columns // parts
    rows = out_ref.shape[0]
    total = (mine_ref[...] + other_ref[...].astype(F32)).astype(BF16)
    row = iota((rows, slots), 0)
    part = row & (parts - 1)
    slot = lax.shift_right_logical(row, parts.bit_length() - 1)
    rank = slot & (capacity - 1)
    source = lax.shift_right_logical(slot, capacity.bit_length() - 1)
    here = iota((rows, slots), 1) == rank * sources + source
    sent = jnp.zeros((rows, width), F32)
    for i in range(parts):
        sent = sent + product(
            one_hot(here & (part == i)), total[:, i * width : (i + 1) * width]
        )
    out_ref[...] = sent.astype(BF16)


def mix_kernel(capacity, parts, parents_here, ids_ref, returned_ref, residual_ref, out_ref):
    children, columns = residual_ref.shape
    width = columns // parts
    rows = returned_ref.shape[0]
    owner, _ = owners(ids_ref[...], parents_here)
    owner_column = as_column(owner)
    square = (children, children)
    earlier = (owner_column == owner) & (iota(square, 1) < iota(square, 0))
    rank = jnp.sum(jnp.where(earlier, 1.0, 0.0), axis=1, keepdims=True)
    slot = (owner_column * capacity + rank).astype(jnp.int32)
    row = iota((children, rows), 1)
    here = lax.shift_right_logical(row, parts.bit_length() - 1) == slot
    part = row & (parts - 1)
    for i in range(parts):
        columns_here = slice(i * width, (i + 1) * width)
        found = product(one_hot(here & (part == i)), returned_ref[...])
        out_ref[:, columns_here] = (
            residual_ref[:, columns_here].astype(F32) + found
        ).astype(BF16)


def local(queries, cached_key_rows, cached_value_rows, parent_ids, lengths, residual, out_weight):
    dp_count = lax.axis_size("dp")
    tensor_count = lax.axis_size("tensor")
    children, columns = queries.shape
    parents_here, prefix, key_columns = cached_key_rows.shape
    kv_heads = key_columns // HEAD_WIDTH
    capacity = max(2, 2 * children // dp_count)
    slots = dp_count * capacity
    width = columns // kv_heads
    message = capacity * kv_heads
    half = out_weight.shape[1] // tensor_count
    parts = 8 // capacity
    ids = parent_ids.reshape(1, children)
    outgoing = pl.pallas_call(
        lambda *refs: send_kernel(capacity, kv_heads, parents_here, *refs),
        out_shape=jax.ShapeDtypeStruct((dp_count * message, width + LANES), BF16),
        in_specs=[VMEM, VMEM],
        out_specs=VMEM,
        compiler_params=PARAMS,
        name="send",
    )(ids, queries)
    arrived = lax.all_to_all(
        outgoing.reshape(dp_count, message, width + LANES), "dp", 0, 0, tiled=True
    ).reshape(dp_count * message, width + LANES)
    places = slots + (parents_here - 1) * CHUNK
    attended, partial_value = pl.pallas_call(
        lambda *refs: attend_kernel(capacity, kv_heads, *refs),
        out_shape=(
            jax.ShapeDtypeStruct((slots, columns), BF16),
            jax.ShapeDtypeStruct((slots, half), BF16),
        ),
        in_specs=[SMEM, VMEM, ANY, ANY, ANY],
        out_specs=(VMEM, VMEM),
        scratch_shapes=[
            pltpu.VMEM((parents_here, prefix, key_columns), BF16),
            pltpu.VMEM((parents_here, prefix, key_columns), BF16),
            pltpu.VMEM((columns, half), BF16),
            pltpu.VMEM((slots, columns), BF16),
            pltpu.VMEM((places, columns), BF16),
            pltpu.VMEM((places, columns), BF16),
            pltpu.SemaphoreType.DMA((3,)),
        ],
        compiler_params=PARAMS,
        name="attend",
    )(lengths, arrived, cached_key_rows, cached_value_rows, out_weight)
    other = lax.ppermute(partial_value, "tensor", [(0, 1), (1, 0)])
    mine = pl.pallas_call(
        project_kernel,
        out_shape=jax.ShapeDtypeStruct((slots, half), F32),
        in_specs=[VMEM, ANY],
        out_specs=VMEM,
        scratch_shapes=[pltpu.VMEM((columns, half), BF16), pltpu.SemaphoreType.DMA((4,))],
        compiler_params=PARAMS,
        cost_estimate=pl.CostEstimate(
            flops=2 * slots * columns * half, bytes_accessed=2 * columns * half, transcendentals=0
        ),
        name="project",
    )(attended, out_weight)
    answers = pl.pallas_call(
        lambda *refs: answer_kernel(capacity, parts, *refs),
        out_shape=jax.ShapeDtypeStruct((slots * parts, half // parts), BF16),
        in_specs=[VMEM, VMEM],
        out_specs=VMEM,
        compiler_params=PARAMS,
        name="answer",
    )(mine, other)
    returned = lax.all_to_all(
        answers.reshape(dp_count, capacity * parts, half // parts), "dp", 0, 0, tiled=True
    ).reshape(slots * parts, half // parts)
    return pl.pallas_call(
        lambda *refs: mix_kernel(capacity, parts, parents_here, *refs),
        out_shape=jax.ShapeDtypeStruct(residual.shape, BF16),
        in_specs=[VMEM, VMEM, VMEM],
        out_specs=VMEM,
        compiler_params=PARAMS,
        name="mix",
    )(ids, returned, residual)


def solution(mesh):
    placed = (
        P("dp", "tensor"),
        P("dp", None, "tensor"),
        P("dp", None, "tensor"),
        P("dp"),
        P("dp"),
        P("dp", "tensor"),
        P("tensor", None),
    )
    return jax.shard_map(
        local, mesh=mesh, in_specs=placed, out_specs=P("dp", "tensor"), check_vma=False
    )
```

time: 137 us -> 104 us (0.76)
  blocking collectives: 43.5 us -> 75.9 us
  Pallas kernels: 0 us -> 23.6 us
  matrix products: 23.4 us -> 0 us
  local copies, waits for them, and re-layouts: 23.4 us -> 0.79 us
  starting transfers between devices: 22.7 us -> 3.36 us
  waiting for transfers between devices: 18.4 us -> 0.01 us
  other arithmetic: 5.04 us -> 0 us
    all_to_all x2, blocking collectives: 43.5 us -> 75.9 us  [the longest x1 49.4 us: local(): lax.all_to_all(outgoing.reshape(dp_count, message, width + LANES), 'dp',...]
    pallas_call x0 -> x5, Pallas kernels: none -> 23.6 us  [the longest x1 10.3 us: local(): pl.pallas_call(lambda *refs: attend_kernel(capacity, kv_heads, *refs), ou...]
    dot_general x6 -> x0, matrix products: 23.4 us -> none  [the longest x2 11 us: attend(): jnp.einsum('sjgd,ljd->jsgl', query_head_count, key_heads, preferred_eleme...]
    all_to_all x2 -> x0, starting transfers between devices: 22.7 us -> none  [the longest x1 16.3 us: local(): lax.all_to_all(slot_parent, 'dp', split_axis=0, concat_axis=0, tiled=True)]
    all_to_all x2 -> x0, waiting for transfers between devices: 18.4 us -> none  [the longest x1 9.86 us: local(): lax.all_to_all(outgoing, 'dp', split_axis=0, concat_axis=0, tiled=True)]
    unnamed x14 -> x2, local copies, waits for them, and re-layouts: 8.25 us -> 0.79 us
    slice x3 -> x0, local copies, waits for them, and re-layouts: 6.34 us -> none  [the longest x1 3.02 us: local(): cached_value_rows[parent]]
    convert_element_type x4 -> x0, local copies, waits for them, and re-layouts: 4.23 us -> none  [attend(): return scaled.reshape(slot_total, columns).astype(jnp.bfloat16)]
  transfers between devices with their start and end apart: 2 -> 1, of which waited for: 2 -> 0; matrix products, arithmetic and copies ran while one was open for 12% -> 0% of each run, Pallas kernels for 0% -> 5%
where the time goes in v1:
time: 104 us
  blocking collectives  75.9 us (73%)
  Pallas kernels  23.6 us (23%)
  starting transfers between devices  3.36 us (3%)
    all_to_all x1, blocking collectives, local(): lax.all_to_all(outgoing.reshape(dp_count, message, width + LANES), 'dp',...  49.4 us
    all_to_all x1, blocking collectives, local(): lax.all_to_all(answers.reshape(dp_count, capacity * parts, half // parts)...  26.4 us
    pallas_call x1, Pallas kernels, local(): pl.pallas_call(lambda *refs: attend_kernel(capacity, kv_heads, *refs), ou...  10.3 us
    pallas_call x1, Pallas kernels, local(): pl.pallas_call(project_kernel, out_shape=jax.ShapeDtypeStruct((slots, hal...  4.87 us
    ppermute x1, starting transfers between devices, local(): other = lax.ppermute(partial_value, 'tensor', [(0, 1), (1, 0)])  3.36 us
    pallas_call x1, Pallas kernels, local(): pl.pallas_call(lambda *refs: send_kernel(capacity, kv_heads, parents_here...  3.01 us
    pallas_call x1, Pallas kernels, local(): pl.pallas_call(lambda *refs: answer_kernel(capacity, parts, *refs), out_s...  2.94 us
    pallas_call x1, Pallas kernels, local(): pl.pallas_call(lambda *refs: mix_kernel(capacity, parts, parents_here, *r...  2.41 us
  transfers between devices with their start and end apart: 1, of which 0 were waited for; matrix products, arithmetic and copies ran while one was open for 0% of the time, Pallas kernels for 5%

profile of v1, /device:TPU:1, one launch (start us, length us, event | category | flops | bytes accessed | tf_op | source)
XLA Modules:
  0.0 103.6 jit_solution(7407178478356088677)
XLA Ops:
  0.0 3.0 %send.1 = bf16[1024,640]{1,0:T(8,128)(2,1)} custom-call(s32[1,128]{1,0:T(1,128)} %bitcast.9, bf16[128,2048]{1,0:T(8,128)(2,1)} %refs_1_.1), custom_call_target="tpu_custom_call" | custom-call | tf_op jit(solution)/shard_map/send/pallas_call | solution.py:245
  3.0 49.4 %all_to_all.10 = bf16[128,8,640]{2,1,0:T(8,128)(2,1)} all-to-all(bf16[128,8,640]{2,1,0:T(8,128)(2,1)} %bitcast.5), channel_id=1, replica_groups=mesh['dp'=128,'tensor'=2] {'dp'}, dimensions={0} | all-to-all | bytes 2621440 | tf_op jit(solution)/shard_map/all_to_all | solution.py:253
  52.5 10.3 %attend.1 = (bf16[256,2048]{1,0:T(8,128)(2,1)}, bf16[256,1024]{1,0:T(8,128)(2,1)}) custom-call(s32[2]{0:T(128)} %refs_0_.1, bf16[1024,640]{1,0:T(8,128)(2,1)} %bitcast.6, bf16[2,1024,512]{2,1,0:T(8,128)(2,1)} %refs_2_.2, bf16[2,1024,512]{2,1,0:T(8,128)(2,1)} %refs_3_.1, bf16[2048,2048]{1,0:T(8,128)(2,1)} %weight_hbm.1), custom_call_target="tpu_custom_call" | custom-call | tf_op jit(solution)/shard_map/attend/pallas_call | solution.py:257
  62.8 3.4 %collective-permute-start = (bf16[256,1024]{1,0:T(8,128)(2,1)}, bf16[256,1024]{1,0:T(8,128)(2,1)S(1)}, u32[]{:S(2)}, u32[]{:S(2)}) collective-permute-start(bf16[256,1024]{1,0:T(8,128)(2,1)} %get-tuple-element.8), channel_id=1, source_target_pairs={{0,1},{1,0},{2,3},{3,2},{4,5},{5,4},{6,7},{7,6},{8,9},{9,8},{10,11... | collective-permute-start | bytes 1572872 | tf_op jit(solution)/shard_map/ppermute | solution.py:277
  66.2 4.9 %project.1.refs_0_ = f32[256,1024]{1,0:T(8,128)} custom-call(bf16[256,2048]{1,0:T(8,128)(2,1)} %get-tuple-element.7.attended_ref, bf16[2048,2048]{1,0:T(8,128)(2,1)} %weight_hbm.1), custom_call_target="tpu_custom_call" | custom-call | flops 1073741824 | bytes 4194304 | tf_op jit(solution)/shard_map/project/pallas_call | solution.py:278
  71.0 0.0 collective-permute-done.refs_1_
  71.0 0.0 copy-start
  71.0 0.8 copy-done
  71.8 2.9 %answer.1 = bf16[1024,256]{1,0:T(8,128)(2,1)} custom-call(f32[256,1024]{1,0:T(8,128)} %project.1.refs_0_, bf16[256,1024]{1,0:T(8,128)(2,1)} %copy-done), custom_call_target="tpu_custom_call" | custom-call | tf_op jit(solution)/shard_map/answer/pallas_call | solution.py:290
  74.8 26.4 %all_to_all.11 = bf16[128,8,256]{2,1,0:T(8,128)(2,1)} all-to-all(bf16[128,8,256]{2,1,0:T(8,128)(2,1)} %bitcast.8), channel_id=1, replica_groups=mesh['dp'=128,'tensor'=2] {'dp'}, dimensions={0} | all-to-all | bytes 1048576 | tf_op jit(solution)/shard_map/all_to_all | solution.py:298
  101.2 2.4 %mix.1 = bf16[128,1024]{1,0:T(8,128)(2,1)} custom-call(s32[1,128]{1,0:T(1,128)} %bitcast.10, bf16[1024,256]{1,0:T(8,128)(2,1)} %bitcast.7, bf16[128,1024]{1,0:T(8,128)(2,1)} %refs_2_.3), custom_call_target="tpu_custom_call" | custom-call | tf_op jit(solution)/shard_map/mix/pallas_call | solution.py:301
Async XLA Ops:
  62.8 8.2 %collective-permute-start = (bf16[256,1024]{1,0:T(8,128)(2,1)}, bf16[256,1024]{1,0:T(8,128)(2,1)S(1)}, u32[]{:S(2)}, u32[]{:S(2)}) collective-permute-start(bf16[256,1024]{1,0:T(8,128)(2,1)} %get-tuple-element.8), channel_id=1, source_target_pairs={{0,1},{1,0},{2,3},{3,2},{4,5},{5,4},{6,7},{7,6},{8,9},{9,8},{10,11... | collective-permute-start | bytes 1572872 | tf_op jit(solution)/shard_map/ppermute | solution.py:277
  71.0 0.8 copy-start

commit v2 on v0

v2 whole, which is shorter than its diff:
```python
import math

import jax
import jax.numpy as jnp
from jax import lax
from jax.experimental import pallas as pl
from jax.experimental.pallas import tpu as pltpu
from jax.sharding import PartitionSpec as P

HEAD_WIDTH = 128
LANES = 128
CHUNK = 64

F32 = jnp.float32
BF16 = jnp.bfloat16
VMEM = pl.BlockSpec(memory_space=pltpu.VMEM)
SMEM = pl.BlockSpec(memory_space=pltpu.SMEM)
HBM = pl.BlockSpec(memory_space=pltpu.HBM)
def params(mib):
    return pltpu.CompilerParams(vmem_limit_bytes=mib * 1024 * 1024)


def iota(shape, dim):
    return lax.broadcasted_iota(jnp.int32, shape, dim)


def one_hot(flags):
    return jnp.where(flags, 1.0, 0.0).astype(BF16)


def product(left, right):
    return jnp.dot(left, right, preferred_element_type=F32)


def as_column(row):
    n = row.shape[1]
    eye = iota((n, n), 0) == iota((n, n), 1)
    return jnp.sum(jnp.where(eye, row, 0.0), axis=1, keepdims=True)


def as_row(column):
    n = column.shape[0]
    eye = iota((n, n), 0) == iota((n, n), 1)
    return jnp.sum(jnp.where(eye, column, 0.0), axis=0, keepdims=True)


def owners(ids, parents_here):
    shift = parents_here.bit_length() - 1
    owner = lax.shift_right_logical(ids, shift)
    return owner.astype(F32), (ids - lax.shift_left(owner, shift)).astype(F32)


def slots_of(ids, parents_here, capacity):
    children = ids.shape[1]
    owner, sub = owners(ids, parents_here)
    square = (children, children)
    earlier = (as_column(owner) == owner) & (iota(square, 0) < iota(square, 1))
    rank = jnp.sum(jnp.where(earlier, 1.0, 0.0), axis=0, keepdims=True)
    return owner * capacity + rank, sub


def send_kernel(capacity, parents_here, ids_ref, queries_ref, out_ref):
    children, columns = queries_ref.shape
    slot, sub = slots_of(ids_ref[...], parents_here, capacity)
    placing = one_hot(iota((out_ref.shape[0], children), 0) == slot.astype(jnp.int32))
    out_ref[:, :columns] = product(placing, queries_ref[...]).astype(BF16)
    mark = jnp.broadcast_to(as_column(sub) + 1.0, (children, LANES)).astype(BF16)
    out_ref[:, columns:] = product(placing, mark).astype(BF16)


def prepare_kernel(lengths_ref, keys_ref, values_ref, turned_ref, valued_ref):
    parents_here, prefix, columns = keys_ref.shape
    for parent in range(parents_here):
        live = iota((prefix, HEAD_WIDTH), 0) < lengths_ref[parent]
        counted = jnp.where(live, 1.0, 0.0).astype(BF16)
        for j in range(columns // HEAD_WIDTH):
            head = slice(j * HEAD_WIDTH, (j + 1) * HEAD_WIDTH)
            turned_ref[parent, j] = keys_ref[parent, :, head].T
            valued_ref[parent, j, :, :HEAD_WIDTH] = jnp.where(
                live, values_ref[parent, :, head].astype(F32), 0.0
            ).astype(BF16)
            valued_ref[parent, j, :, HEAD_WIDTH:] = counted


def attend_kernel(
    lengths_ref, arrived_ref, turned_ref, valued_hbm, weight_hbm,
    attended_ref, partial_ref, mine_ref, valued_ref, weight_ref, ordered, answered, sems,
):
    parents_here, kv_heads, _, prefix = turned_ref.shape
    slots, columns = attended_ref.shape
    width = columns // kv_heads
    group = width // HEAD_WIDTH
    half = partial_ref.shape[1]
    core = lax.axis_index("tensor")
    mine = pl.multiple_of(core * half, half)
    other = pl.multiple_of((1 - core) * half, half)
    copies = (
        pltpu.make_async_copy(valued_hbm, valued_ref, sems.at[0]),
        pltpu.make_async_copy(weight_hbm.at[:, pl.ds(other, half)], weight_ref, sems.at[1]),
        pltpu.make_async_copy(weight_hbm.at[:, pl.ds(mine, half)], mine_ref, sems.at[2]),
    )
    copies[0].start()
    arrived = arrived_ref[...].reshape(slots, arrived_ref.shape[2])
    marks = arrived[:, columns:].astype(F32)
    before = one_hot(iota((slots, slots), 0) > iota((slots, slots), 1))
    position = jnp.full((slots, LANES), -1.0, F32)
    start = jnp.int32(0)
    ends = []
    for parent in range(parents_here):
        mine = marks == parent + 1.0
        ahead = product(before, one_hot(mine))
        position = jnp.where(mine, ahead + start.astype(F32), position)
        count = (jnp.sum(jnp.where(mine, 1.0, 0.0)) * (1.0 / LANES)).astype(jnp.int32)
        start = start + lax.shift_left(
            lax.shift_right_logical(count + (CHUNK - 1), CHUNK.bit_length() - 1),
            CHUNK.bit_length() - 1,
        )
        ends.append(start)
    position_row = jnp.concatenate(
        [as_row(position[i : i + LANES]) for i in range(0, slots, LANES)], axis=1
    ).astype(jnp.int32)
    places = ordered.shape[0]
    ordering = one_hot(iota((places, slots), 0) == position_row)
    ordered[...] = product(ordering, arrived[:, :columns]).astype(BF16)
    answered[...] = jnp.zeros_like(answered)
    copies[0].wait()
    copies[1].start()
    copies[2].start()
    factor = (1.0 / math.sqrt(HEAD_WIDTH))

    def chunk_step(index, carry):
        base = pl.multiple_of(index * CHUNK, CHUNK)
        parent = jnp.int32(0)
        for end in ends[:-1]:
            parent = parent + (base >= end).astype(jnp.int32)
        length = lengths_ref[parent]

        def heads_of(span):
            for j in range(kv_heads):
                block = ordered[pl.ds(base, CHUNK), j * width : (j + 1) * width]
                heads = jnp.concatenate(
                    [block[:, g * HEAD_WIDTH : (g + 1) * HEAD_WIDTH] for g in range(group)], axis=0
                )
                scores = product(heads, turned_ref[parent, j, :, :span])
                raised = jnp.exp(scores * factor).astype(BF16)
                summed = product(raised, valued_ref[parent, j, :span])
                scaled = (summed[:, :HEAD_WIDTH] / summed[:, HEAD_WIDTH:]).astype(BF16)
                for g in range(group):
                    answered[
                        pl.ds(base, CHUNK),
                        j * width + g * HEAD_WIDTH : j * width + (g + 1) * HEAD_WIDTH,
                    ] = scaled[g * CHUNK : (g + 1) * CHUNK]

        for span in range(256, prefix + 1, 256):
            @pl.when((length > span - 256) & (length <= span))
            def _(span=span):
                heads_of(span)
        return carry

    lax.fori_loop(0, lax.shift_right_logical(start, CHUNK.bit_length() - 1), chunk_step, 0)
    lane = iota((slots, places), 1).astype(F32)
    back = one_hot(lane == position[:, :1])
    attended_ref[...] = product(back, answered[...]).astype(BF16)
    copies[1].wait()
    partial_ref[...] = product(attended_ref[...], weight_ref[...]).astype(BF16)
    copies[2].wait()


def project_kernel(attended_ref, weight_ref, out_ref):
    out_ref[...] = product(attended_ref[...], weight_ref[...])


def mix_kernel(capacity, parents_here, ids_ref, returned_ref, residual_ref, out_ref):
    children = residual_ref.shape[0]
    slot, _ = slots_of(ids_ref[...], parents_here, capacity)
    placing = one_hot(
        iota((children, returned_ref.shape[0]), 1) == as_column(slot).astype(jnp.int32)
    )
    found = product(placing, returned_ref[...])
    out_ref[...] = (residual_ref[...].astype(F32) + found).astype(BF16)


def local(queries, cached_key_rows, cached_value_rows, parent_ids, lengths, residual, out_weight):
    dp_count = lax.axis_size("dp")
    tensor_count = lax.axis_size("tensor")
    children, columns = queries.shape
    parents_here, prefix, key_columns = cached_key_rows.shape
    kv_heads = key_columns // HEAD_WIDTH
    capacity = max(2, 2 * children // dp_count)
    slots = dp_count * capacity
    half = out_weight.shape[1] // tensor_count
    ids = parent_ids.reshape(1, children)
    outgoing = pl.pallas_call(
        lambda *refs: send_kernel(capacity, parents_here, *refs),
        out_shape=jax.ShapeDtypeStruct((slots, columns + LANES), BF16),
        in_specs=[VMEM, VMEM],
        out_specs=VMEM,
        compiler_params=params(6),
        name="send",
    )(ids, queries)
    arrived = lax.all_to_all(
        outgoing.reshape(dp_count, capacity, columns + LANES), "dp", 0, 0, tiled=True
    )
    turned, valued = pl.pallas_call(
        prepare_kernel,
        out_shape=(
            jax.ShapeDtypeStruct((parents_here, kv_heads, HEAD_WIDTH, prefix), BF16),
            jax.ShapeDtypeStruct((parents_here, kv_heads, prefix, 2 * HEAD_WIDTH), BF16),
        ),
        in_specs=[SMEM, VMEM, VMEM],
        out_specs=(VMEM, VMEM),
        compiler_params=params(16),
        cost_estimate=pl.CostEstimate(
            flops=10000000000, bytes_accessed=4 * out_weight.size, transcendentals=0
        ),
        name="prepare",
    )(lengths, cached_key_rows, cached_value_rows)
    places = slots + (parents_here - 1) * CHUNK
    attended, partial_value, weight_mine = pl.pallas_call(
        attend_kernel,
        out_shape=(
            jax.ShapeDtypeStruct((slots, columns), BF16),
            jax.ShapeDtypeStruct((slots, half), BF16),
            jax.ShapeDtypeStruct((columns, half), BF16),
        ),
        in_specs=[SMEM, VMEM, VMEM, HBM, HBM],
        out_specs=(VMEM, VMEM, VMEM),
        scratch_shapes=[
            pltpu.VMEM((parents_here, kv_heads, prefix, 2 * HEAD_WIDTH), BF16),
            pltpu.VMEM((columns, half), BF16),
            pltpu.VMEM((places, columns), BF16),
            pltpu.VMEM((places, columns), BF16),
            pltpu.SemaphoreType.DMA((3,)),
        ],
        compiler_params=params(40),
        name="attend",
    )(
        lengths,
        arrived,
        turned,
        pltpu.with_memory_space_constraint(valued, pltpu.HBM),
        pltpu.with_memory_space_constraint(out_weight, pltpu.HBM),
    )
    other = lax.ppermute(partial_value, "tensor", [(0, 1), (1, 0)])
    mine = pl.pallas_call(
        project_kernel,
        out_shape=jax.ShapeDtypeStruct((slots, half), F32),
        in_specs=[VMEM, VMEM],
        out_specs=VMEM,
        compiler_params=params(14),
        cost_estimate=pl.CostEstimate(
            flops=2 * slots * columns * half, bytes_accessed=2 * columns * half, transcendentals=0
        ),
        name="project",
    )(attended, weight_mine)
    answers = (mine + other.astype(F32)).astype(BF16)
    returned = lax.all_to_all(
        answers.reshape(dp_count, capacity, half), "dp", 0, 0, tiled=True
    ).reshape(slots, half)
    return pl.pallas_call(
        lambda *refs: mix_kernel(capacity, parents_here, *refs),
        out_shape=jax.ShapeDtypeStruct(residual.shape, BF16),
        in_specs=[VMEM, VMEM, VMEM],
        out_specs=VMEM,
        compiler_params=params(6),
        name="mix",
    )(ids, returned, residual)


def solution(mesh):
    placed = (
        P("dp", "tensor"),
        P("dp", None, "tensor"),
        P("dp", None, "tensor"),
        P("dp"),
        P("dp"),
        P("dp", "tensor"),
        P("tensor", None),
    )
    return jax.shard_map(
        local, mesh=mesh, in_specs=placed, out_specs=P("dp", "tensor"), check_vma=False
    )
```

time: 137 us -> 91.2 us (0.67)
  matrix products: 23.4 us -> 0 us
  blocking collectives: 43.5 us -> 25 us
  Pallas kernels: 0 us -> 15.5 us
  local copies, waits for them, and re-layouts: 23.4 us -> 8.5 us
  other arithmetic: 5.04 us -> 0.16 us
  waiting for transfers between devices: 18.4 us -> 21.4 us
  starting transfers between devices: 22.7 us -> 20.2 us
    dot_general x6 -> x0, matrix products: 23.4 us -> none  [the longest x2 11 us: attend(): jnp.einsum('sjgd,ljd->jsgl', query_head_count, key_heads, preferred_eleme...]
    all_to_all x2 -> x1, blocking collectives: 43.5 us -> 25 us  [local(): lax.all_to_all(answers.reshape(dp_count, capacity, half), 'dp', 0, 0, til...]
    pallas_call x0 -> x5, Pallas kernels: none -> 15.5 us  [the longest x1 10.2 us: local(): pl.pallas_call(attend_kernel, out_shape=(jax.ShapeDtypeStruct((slots, col...]
    all_to_all x2 -> x1, starting transfers between devices: 22.7 us -> 16.3 us  [local(): lax.all_to_all(outgoing.reshape(dp_count, capacity, columns + LANES), 'dp...]
    slice x3 -> x0, local copies, waits for them, and re-layouts: 6.34 us -> none  [the longest x1 3.02 us: local(): cached_value_rows[parent]]
    convert_element_type x4 -> x0, local copies, waits for them, and re-layouts: 4.23 us -> none  [attend(): return scaled.reshape(slot_total, columns).astype(jnp.bfloat16)]
    ppermute x0 -> x1, starting transfers between devices: none -> 3.91 us  [local(): other = lax.ppermute(partial_value, 'tensor', [(0, 1), (1, 0)])]
    all_to_all x2 -> x1, waiting for transfers between devices: 18.4 us -> 21.1 us  [local(): lax.all_to_all(outgoing.reshape(dp_count, capacity, columns + LANES), 'dp...]
  transfers between devices with their start and end apart: 2 -> 2, of which waited for: 2 -> 2; matrix products, arithmetic and copies ran while one was open for 12% -> 0% of each run, Pallas kernels for 0% -> 4%
where the time goes in v2:
time: 91.2 us; the launch traced here: 90.9 us
  blocking collectives  25 us (27%)
  waiting for transfers between devices  21.4 us (23%)
  starting transfers between devices  20.2 us (22%)
  Pallas kernels  15.5 us (17%)
  local copies, waits for them, and re-layouts  8.5 us (9%)
    all_to_all x1, blocking collectives, local(): lax.all_to_all(answers.reshape(dp_count, capacity, half), 'dp', 0, 0, til...  25 us
    all_to_all x1, waiting for transfers between devices, local(): lax.all_to_all(outgoing.reshape(dp_count, capacity, columns + LANES), 'dp...  21.1 us
    all_to_all x1, starting transfers between devices, local(): lax.all_to_all(outgoing.reshape(dp_count, capacity, columns + LANES), 'dp...  16.3 us
    pallas_call x1, Pallas kernels, local(): pl.pallas_call(attend_kernel, out_shape=(jax.ShapeDtypeStruct((slots, col...  10.2 us
    unnamed x16, local copies, waits for them, and re-layouts  6.84 us
    ppermute x1, starting transfers between devices, local(): other = lax.ppermute(partial_value, 'tensor', [(0, 1), (1, 0)])  3.91 us
    pallas_call x1, Pallas kernels, local(): pl.pallas_call(prepare_kernel, out_shape=(jax.ShapeDtypeStruct((parents_h...  2.39 us
  transfers between devices with their start and end apart: 2, of which 2 were waited for; matrix products, arithmetic and copies ran while one was open for 0% of the time, Pallas kernels for 4%

profile of v2, /device:TPU:1, one launch (start us, length us, event | category | flops | bytes accessed | tf_op | source)
XLA Modules:
  0.0 90.9 jit_solution(3151432697102675352)
XLA Ops:
  0.0 1.0 %copy-done.1 = bf16[128,2048]{1,0:T(8,128)(2,1)S(1)} copy-done((bf16[128,2048]{1,0:T(8,128)(2,1)S(1)}, bf16[128,2048]{1,0:T(8,128)(2,1)}, u32[]{:S(2)}) %copy-start.1) | copy-done | bytes 524312
  1.0 0.7 copy-done.3
  1.7 0.5 send.1
  2.2 0.0 copy-start.5
  2.2 1.3 %reshape.13 = bf16[128,2,2176]{2,1,0:T(2,128)(2,1)} reshape(bf16[256,2176]{1,0:T(8,128)(2,1)S(1)} %send.1) | data formatting | bytes 2228224 | tf_op jit(solution)/shard_map/reshape | solution.py:202
  3.5 16.3 %all-to-all-start = ((bf16[128,2,2176]{2,1,0:T(2,128)(2,1)}), bf16[128,2,2176]{2,1,0:T(2,128)(2,1)S(1)}, u32[]{:S(2)}, u32[]{:S(2)}) async-start(bf16[128,2,2176]{2,1,0:T(2,128)(2,1)} %reshape.13), calls=%async_computation | async-start | bytes 2228224 | tf_op jit(solution)/shard_map/all_to_all | solution.py:201
  19.9 0.0 copy-done.5
  19.9 0.0 copy-start.6
  19.9 1.6 %copy-done.6 = bf16[2,1024,512]{2,1,0:T(8,128)(2,1)S(1)} copy-done((bf16[2,1024,512]{2,1,0:T(8,128)(2,1)S(1)}, bf16[2,1024,512]{2,1,0:T(8,128)(2,1)}, u32[]{:S(2)}) %copy-start.6) | copy-done | bytes 2097176
  21.5 1.6 %copy-done.7 = bf16[2,1024,512]{2,1,0:T(8,128)(2,1)S(1)} copy-done((bf16[2,1024,512]{2,1,0:T(8,128)(2,1)S(1)}, bf16[2,1024,512]{2,1,0:T(8,128)(2,1)}, u32[]{:S(2)}) %copy-start.7) | copy-done | bytes 2097176
  23.0 2.4 %prepare.1 = (bf16[2,4,128,1024]{3,2,1,0:T(8,128)(2,1)S(1)}, bf16[2,4,1024,256]{3,2,1,0:T(8,128)(2,1)S(1)}) custom-call(s32[2]{0:T(128)S(1)} %copy-done.5, bf16[2,1024,512]{2,1,0:T(8,128)(2,1)S(1)} %copy-done.6, bf16[2,1024,512]{2,1,0:T(8,128)(2,1)S(1)} %copy-done.7), custom_call_target="tpu_custom_call" | custom-call | flops 10000000000 | bytes 16777216 | tf_op jit(solution)/shard_map/prepare/pallas_call | solution.py:204
  25.5 1.9 %copy-done = bf16[2,4,1024,256]{3,2,1,0:T(8,128)(2,1)} copy-done((bf16[2,4,1024,256]{3,2,1,0:T(8,128)(2,1)}, bf16[2,4,1024,256]{3,2,1,0:T(8,128)(2,1)S(1)}, u32[]{:S(2)}) %copy-start) | copy-done | bytes 4194328
  27.4 21.1 %all-to-all-done.arrived_ref = bf16[128,2,2176]{2,1,0:T(2,128)(2,1)S(1)} async-done(((bf16[128,2,2176]{2,1,0:T(2,128)(2,1)}), bf16[128,2,2176]{2,1,0:T(2,128)(2,1)S(1)}, u32[]{:S(2)}, u32[]{:S(2)}) %all-to-all-start) | async-done | bytes 1114144 | tf_op jit(solution)/shard_map/all_to_all | solution.py:201
  48.5 10.2 %attend.1 = (bf16[256,2048]{1,0:T(8,128)(2,1)S(1)}, bf16[256,1024]{1,0:T(8,128)(2,1)S(1)}, bf16[2048,1024]{1,0:T(8,128)(2,1)S(1)}) custom-call(s32[2]{0:T(128)S(1)} %copy-done.5, bf16[128,2,2176]{2,1,0:T(2,128)(2,1)S(1)} %all-to-all-done.arrived_ref, bf16[2,4,128,1024]{3,2,1,0:T(8,128)(2,1)S(1)} %get-tuple-element.10.turned_ref, ...), custom_call_target="tpu_custom_call" | custom-call | tf_op jit(solution)/shard_map/attend/pallas_call | solution.py:219
  58.8 3.9 %collective-permute-start = (bf16[256,1024]{1,0:T(8,128)(2,1)S(1)}, bf16[256,1024]{1,0:T(8,128)(2,1)S(1)}, u32[]{:S(2)}, u32[]{:S(2)}) collective-permute-start(bf16[256,1024]{1,0:T(8,128)(2,1)S(1)} %get-tuple-element.14), channel_id=1, source_target_pairs={{0,1},{1,0},{2,3},{3,2},{4,5},{5,4},{6,7},{7,6},{8,9},{9,8},{10,11... | collective-permute-start | bytes 1572872 | tf_op jit(solution)/shard_map/ppermute | solution.py:244
  62.7 1.2 %project.1 = f32[256,1024]{1,0:T(8,128)S(1)} custom-call(bf16[256,2048]{1,0:T(8,128)(2,1)S(1)} %get-tuple-element.12.attended_ref, bf16[2048,1024]{1,0:T(8,128)(2,1)S(1)} %get-tuple-element.13.weight_ref), custom_call_target="tpu_custom_call" | custom-call | flops 1073741824 | bytes 4194304 | tf_op jit(solution)/shard_map/project/pallas_call | solution.py:245
  63.9 0.3 collective-permute-done
  64.2 0.2 add_convert_fusion
  64.4 0.0 copy-start.2
  64.4 0.0 copy-start.4
  64.4 0.2 reshape.14
  64.6 25.0 %all_to_all.10 = bf16[128,2,1024]{2,1,0:T(2,128)(2,1)S(1)} all-to-all(bf16[128,2,1024]{2,1,0:T(2,128)(2,1)S(1)} %reshape.14), channel_id=1, replica_groups=mesh['dp'=128,'tensor'=2] {'dp'}, dimensions={0} | all-to-all | bytes 1048576 | tf_op jit(solution)/shard_map/all_to_all | solution.py:257
  89.6 0.2 reshape.15.refs_1_
  89.8 1.1 %mix.1 = bf16[128,1024]{1,0:T(8,128)(2,1)} custom-call(s32[1,128]{1,0:T(1,128)S(1)} %bitcast.2, bf16[256,1024]{1,0:T(8,128)(2,1)S(1)} %reshape.15.refs_1_, bf16[128,1024]{1,0:T(8,128)(2,1)S(1)} %copy-done.2), custom_call_target="tpu_custom_call" | custom-call | tf_op jit(solution)/shard_map/mix/pallas_call | solution.py:260
  (6 shorter events, 0.0 us)
Async XLA Ops:
  0.0 1.0 %copy-start.1 = (bf16[128,2048]{1,0:T(8,128)(2,1)S(1)}, bf16[128,2048]{1,0:T(8,128)(2,1)}, u32[]{:S(2)}) copy-start(bf16[128,2048]{1,0:T(8,128)(2,1)} %refs_1_.1) | copy-start | bytes 1572868
  1.0 0.7 copy-start.3
  2.2 17.6 %copy-start.5 = (s32[2]{0:T(128)S(1)}, s32[2]{0:T(128)}, u32[]{:S(2)}) copy-start(s32[2]{0:T(128)} %lengths_ref.3) | copy-start | bytes 28
  3.5 45.0 %all-to-all-start = ((bf16[128,2,2176]{2,1,0:T(2,128)(2,1)}), bf16[128,2,2176]{2,1,0:T(2,128)(2,1)S(1)}, u32[]{:S(2)}, u32[]{:S(2)}) async-start(bf16[128,2,2176]{2,1,0:T(2,128)(2,1)} %reshape.13), calls=%async_computation | async-start | bytes 2228224 | tf_op jit(solution)/shard_map/all_to_all | solution.py:201
  19.9 1.6 %copy-start.6 = (bf16[2,1024,512]{2,1,0:T(8,128)(2,1)S(1)}, bf16[2,1024,512]{2,1,0:T(8,128)(2,1)}, u32[]{:S(2)}) copy-start(bf16[2,1024,512]{2,1,0:T(8,128)(2,1)} %keys_ref.1) | copy-start | bytes 6291460
  21.5 1.6 %copy-start.7 = (bf16[2,1024,512]{2,1,0:T(8,128)(2,1)S(1)}, bf16[2,1024,512]{2,1,0:T(8,128)(2,1)}, u32[]{:S(2)}) copy-start(bf16[2,1024,512]{2,1,0:T(8,128)(2,1)} %values_ref.1) | copy-start | bytes 6291460
  25.4 2.0 %copy-start = (bf16[2,4,1024,256]{3,2,1,0:T(8,128)(2,1)}, bf16[2,4,1024,256]{3,2,1,0:T(8,128)(2,1)S(1)}, u32[]{:S(2)}) copy-start(bf16[2,4,1024,256]{3,2,1,0:T(8,128)(2,1)S(1)} %get-tuple-element.11.valued_hbm) | copy-start | bytes 12582916
  58.8 5.4 %collective-permute-start = (bf16[256,1024]{1,0:T(8,128)(2,1)S(1)}, bf16[256,1024]{1,0:T(8,128)(2,1)S(1)}, u32[]{:S(2)}, u32[]{:S(2)}) collective-permute-start(bf16[256,1024]{1,0:T(8,128)(2,1)S(1)} %get-tuple-element.14), channel_id=1, source_target_pairs={{0,1},{1,0},{2,3},{3,2},{4,5},{5,4},{6,7},{7,6},{8,9},{9,8},{10,11... | collective-permute-start | bytes 1572872 | tf_op jit(solution)/shard_map/ppermute | solution.py:244
  64.4 25.4 %copy-start.2 = (bf16[128,1024]{1,0:T(8,128)(2,1)S(1)}, bf16[128,1024]{1,0:T(8,128)(2,1)}, u32[]{:S(2)}) copy-start(bf16[128,1024]{1,0:T(8,128)(2,1)} %refs_2_.1) | copy-start | bytes 786436
  64.4 25.4 %copy-start.4 = (s32[128]{0:T(128)S(1)}, s32[128]{0:T(128)}, u32[]{:S(2)}) copy-start(s32[128]{0:T(128)} %param.10) | copy-start | bytes 1540
